TPU v7x, 32 devices: a whole 2x2x4 slice. The times are simulated.
32 devices in a mesh: row: 4 (over y, core), col: 8 (over z, x).
Axes of the slice: x: 2, y: 2, z: 4, core: 2. Of those that a mesh axis runs over, the one named last changes fastest.
Arguments:
- left_derivatives: bfloat16 [256, 512, 512], P(('row', 'col')), may hold values from -0.25 to 0.25
- right_derivatives: bfloat16 [256, 512, 512], P(('row', 'col')), may hold values from -0.25 to 0.25
- bundle_tile_slot: int32 [256], P(('row', 'col')), may hold values from 0 to 511, as said below
- tile_pos: int32 [4, 8, 16], P('row', 'col'), may hold values from 0 to 511, as said below
- right_sides: float32 [16, 65536], P(None, ('row', 'col')), may hold values from -6 to 6
- diagonal: float32 [65536], P(('row', 'col')), may hold values from 0.8 to 3
Outputs:
- solution: float32 [16, 65536], P(None, ('row', 'col'))
Inputs may be any that keep to these rules, and one draw needn't show every extreme that they name: `bundle_tile_slot`: bundle b lies on the device of index b // 8 along row+col. The slot g that it names belongs to a device of the same row index. Of the bundles of one device, at most 2 name slots of any one device, and in each row some device is named exactly 2 times by the bundles of every device of that row. `tile_pos`: the 16 entries of one device are distinct.
All inputs are finite; a program needn't handle non-finite values.
Results may differ from a plain program's by a relative error of at most 0.002.
Values may be sent and summed in bfloat16 or wider, within the bound.
A program may use at most 192 MiB of HBM per device.

v0:
```python
import jax
import jax.numpy as jnp
from jax import lax
from jax.sharding import PartitionSpec as P

BLOCK_PARAMS = 512
NRHS = 16
BLK_DEV = 4
CAP = 16
SEND_CAP = 2
ITERS = 3


highest = lax.Precision.HIGHEST


def route_plan(bundle_tile_slot):
    column_count = lax.axis_size("col")
    owner_column = bundle_tile_slot // CAP % column_count
    target = bundle_tile_slot % CAP
    number = bundle_tile_slot.shape[0]
    serial = jnp.arange(number, dtype=jnp.int32)
    same_owner = owner_column[:, None] == owner_column[None, :]
    earlier = serial[None, :] < serial[:, None]
    rank_in = jnp.sum(jnp.logical_and(same_owner, earlier).astype(jnp.int32), axis=1)
    placing = owner_column * SEND_CAP + rank_in
    capacity = column_count * SEND_CAP
    chosen = placing[None, :] == jnp.arange(capacity, dtype=jnp.int32)[:, None]
    filled = jnp.any(chosen, axis=1)
    source = jnp.sum(jnp.where(chosen, serial[None, :], 0), axis=1)
    labels = jnp.sum(jnp.where(chosen, target[None, :], 0), axis=1)
    labels = jnp.where(filled, labels, -1)
    return (source, filled, labels.reshape(column_count, SEND_CAP))


def pack_slots(values, source, filled):
    picked = jnp.take(values, source, axis=0)
    mask_shape = (filled.shape[0],) + (1,) * (values.ndim - 1)
    picked = jnp.where(filled.reshape(mask_shape), picked, jnp.zeros((), values.dtype))
    return picked.reshape((-1, SEND_CAP) + values.shape[1:])


def collect_tiles(gram_tiles, labels):
    flat_labels = labels.reshape(-1)
    selector = (flat_labels[:, None] == jnp.arange(CAP, dtype=jnp.int32)[None, :]).astype(
        jnp.bfloat16
    )
    stacked = gram_tiles.reshape(flat_labels.shape[0], BLOCK_PARAMS * BLOCK_PARAMS)
    summed = jnp.dot(selector.T, stacked, preferred_element_type=jnp.float32)
    return summed.reshape(CAP, BLOCK_PARAMS, BLOCK_PARAMS)


def tile_places(tile_pos):
    column_span = lax.axis_size("row") * BLK_DEV
    position = tile_pos.reshape(-1)
    return (position // column_span, position % column_span)


def local_products(matrix, row_place, column_place, row_view, column_view):
    band_view = row_view.reshape(NRHS, -1, BLOCK_PARAMS)
    cross_view = column_view.reshape(NRHS, -1, BLOCK_PARAMS)
    pick_rows = jax.nn.one_hot(row_place, band_view.shape[1], dtype=jnp.float32)
    pick_columns = jax.nn.one_hot(column_place, cross_view.shape[1], dtype=jnp.float32)
    at_columns = jnp.einsum("sm,rmb->rsb", pick_columns, cross_view, precision=highest)
    at_rows = jnp.einsum("si,ria->rsa", pick_rows, band_view, precision=highest)
    row_terms = jnp.einsum("rsb,sab->rsa", at_columns, matrix, precision=highest)
    column_terms = jnp.einsum("rsa,sab->rsb", at_rows, matrix, precision=highest)
    rows_part = jnp.einsum("si,rsa->ria", pick_rows, row_terms, precision=highest)
    columns_part = jnp.einsum("sm,rsb->rmb", pick_columns, column_terms, precision=highest)
    return (rows_part.reshape(NRHS, -1), columns_part.reshape(NRHS, -1))


def solve(initial, operate, combine_sums):

    def inner(pairs):
        partial_value = jnp.stack(
            [jnp.sum(first_side * second_side, axis=1) for first_side, second_side in pairs]
        )
        return combine_sums(partial_value)

    count_rhs = initial.shape[0]
    beta_now = jnp.sqrt(inner([(initial, initial)])[0])
    beta_old = jnp.zeros((count_rhs,), jnp.float32)
    lanczos_old = initial
    lanczos_now = initial
    delta_bar = jnp.zeros((count_rhs,), jnp.float32)
    epsilon_now = jnp.zeros((count_rhs,), jnp.float32)
    phi_bar = beta_now
    cosine = -jnp.ones((count_rhs,), jnp.float32)
    sine_now = jnp.zeros((count_rhs,), jnp.float32)
    search_now = jnp.zeros_like(initial)
    search_old = jnp.zeros_like(initial)
    solution = jnp.zeros_like(initial)
    for iteration in range(ITERS):
        basis = lanczos_now / beta_now[:, None]
        image = operate(basis)
        if iteration > 0:
            image = image - (beta_now / beta_old)[:, None] * lanczos_old
        alpha_now = inner([(basis, image)])[0]
        image = image - (alpha_now / beta_now)[:, None] * lanczos_now
        beta_next = jnp.sqrt(inner([(image, image)])[0])
        lanczos_old, lanczos_now = (lanczos_now, image)
        beta_old, beta_now = (beta_now, beta_next)
        epsilon_old = epsilon_now
        delta_now = cosine * delta_bar + sine_now * alpha_now
        gamma_bar = sine_now * delta_bar - cosine * alpha_now
        epsilon_now = sine_now * beta_now
        delta_bar = -cosine * beta_now
        gamma_now = jnp.sqrt(gamma_bar * gamma_bar + beta_now * beta_now)
        cosine = gamma_bar / gamma_now
        sine_now = beta_now / gamma_now
        phi_now = cosine * phi_bar
        phi_bar = sine_now * phi_bar
        search_older, search_old = (search_old, search_now)
        search_now = (
            basis - epsilon_old[:, None] * search_older - delta_now[:, None] * search_old
        ) / gamma_now[:, None]
        solution = solution + phi_now[:, None] * search_now
    return solution


def body(left_derivatives, right_derivatives, bundle_tile_slot, tile_pos, right_sides, diagonal):
    source, filled, labels = route_plan(bundle_tile_slot)
    local_gram_tiles = jnp.einsum(
        "nma,nmb->nab", left_derivatives, right_derivatives, preferred_element_type=jnp.float32
    ).astype(jnp.bfloat16)
    gram_tiles, arrived = (
        lax.all_to_all(
            pack_slots(local_gram_tiles, source, filled),
            "col",
            split_axis=0,
            concat_axis=0,
            tiled=True,
        ),
        lax.all_to_all(labels, "col", split_axis=0, concat_axis=0, tiled=True),
    )
    matrix = collect_tiles(gram_tiles, arrived)
    row_place, column_place = tile_places(tile_pos)
    initial, diagonal_band = (
        lax.all_gather(right_sides, "col", axis=1, tiled=True),
        lax.all_gather(diagonal, "col", axis=0, tiled=True),
    )
    column_index = lax.axis_index("col")
    own_width = BLK_DEV * BLOCK_PARAMS

    def operate_bands(vector):
        own_block = lax.dynamic_slice_in_dim(vector, column_index * own_width, own_width, 1)
        column_view = lax.all_gather(
            own_block.astype(jnp.bfloat16), "row", axis=1, tiled=True
        ).astype(own_block.dtype)
        rows_part, columns_part = local_products(
            matrix, row_place, column_place, vector, column_view
        )
        from_rows = lax.psum(rows_part.astype(jnp.bfloat16), "col").astype(jnp.float32)
        own_columns = lax.psum_scatter(columns_part, "row", scatter_dimension=1, tiled=True)
        from_columns = lax.all_gather(own_columns, "col", axis=1, tiled=True)
        return from_rows + from_columns + diagonal_band[None, :] * vector

    def band_totals(partial_value):
        return lax.psum(partial_value, "row")

    solution_band = solve(initial, operate_bands, band_totals)
    return lax.dynamic_slice_in_dim(solution_band, column_index * own_width, own_width, 1)


def solution(mesh):
    placed = (
        P(("row", "col"), None, None),
        P(("row", "col"), None, None),
        P(("row", "col")),
        P("row", "col", None),
        P(None, ("row", "col")),
        P(("row", "col")),
    )
    return jax.shard_map(
        body, mesh=mesh, in_specs=placed, out_specs=P(None, ("row", "col")), check_vma=False
    )
```

profile of v0, /device:TPU:0, one launch (start us, length us, event | category | flops | bytes accessed | tf_op | source)
XLA Modules:
  0.0 842.5 jit_solution(159011133607835245)
XLA Ops:
  8.3 7.3 all-to-all-start
  15.7 7.8 convolution_convert_fusion
  23.5 6.8 gather_fusion
  30.3 7.6 select_select_fusion
  37.9 6.2 all-to-all-start.1
  46.2 193.7 %all-gather.5.cloned.1.call-done = f32[16,16384]{1,0:T(8,128)} async-done(((f32[16,2048]{1,0:T(8,128)}), f32[16,16384]{1,0:T(8,128)}) %all-gather.5.cloned.1.call-update) | async-done | bytes 1048592 | tf_op jit(solution)/shard_map/all_gather | solution.py:140
  239.9 1.5 multiply_reduce_fusion.6
  241.4 5.7 psum.70
  247.0 1.4 broadcast_divide_fusion.2
  248.4 6.0 all_gather.25
  255.6 9.1 %fusion.12 = f32[16,512,512]{2,0,1:T(8,128)S(1)} fusion(s32[16]{0:T(128)S(1)} %eq.120, bf16[2,8,512,512]{3,2,1,0:T(8,128)(2,1)} %bitcast.44), kind=kOutput, calls=%fused_computation.13 | convolution fusion | flops 134217984 | bytes 25165888 | tf_op jit(solution)/shard_map/dot_general | solution.py:49
  264.8 19.0 %fusion.18 = f32[16,16,512]{2,0,1:T(8,128)S(1)} fusion(f32[16,512,512]{2,0,1:T(8,128)S(1)} %fusion.12, f32[16,16,512]{2,1,0:T(8,128)S(1)} %convolution_bitcast_fusion.2), kind=kOutput, calls=%fused_computation.22 | convolution fusion | flops 805306368 | bytes 17825792 | tf_op jit(solution)/shard_map/rsa,sab->rsb/dot_general | solution.py:67
  284.5 1.1 copy.70
  286.0 30.1 %fusion.15 = f32[16,16,512]{2,0,1:T(8,128)S(1)} fusion(f32[16,512,512]{2,0,1:T(8,128)} %copy-done, f32[16,16,512]{2,1,0:T(8,128)S(1)} %convolution_bitcast_fusion.5), kind=kOutput, calls=%fused_computation.21 | convolution fusion | flops 805306368 | bytes 17825792 | tf_op jit(solution)/shard_map/rsb,sab->rsa/dot_general | solution.py:66
  316.1 0.9 convolution_convert_fusion.3
  317.0 1.1 copy.68
  318.7 30.6 %all_gather.27 = f32[16384]{0:T(1024)S(1)} all-gather(f32[2048]{0:T(1024)S(1)} %copy-done.3), channel_id=1, replica_groups=mesh['row'=4,'col'=8] {'col'}, dimensions={0}, use_global_device_ids=true | all-gather | bytes 73728 | tf_op jit(solution)/shard_map/all_gather | solution.py:141
  349.4 38.9 %all-reduce.4.cloned.1.call-done = bf16[16,16384]{1,0:T(8,128)(2,1)} async-done(((bf16[16,16384]{1,0:T(8,128)(2,1)}), bf16[16,16384]{1,0:T(8,128)(2,1)}) %all-reduce.4.cloned.1.call-update) | async-done | bytes 524304 | tf_op jit(solution)/shard_map/psum | solution.py:154
  388.3 41.5 %all-gather.7.cloned.1.call-done = f32[16,16384]{1,0:T(8,128)} async-done(((f32[16,2048]{1,0:T(8,128)}), f32[16,16384]{1,0:T(8,128)}) %all-gather.7.cloned.1.call-update) | async-done | bytes 1048592 | tf_op jit(solution)/shard_map/all_gather | solution.py:156
  429.8 1.8 multiply_reduce_fusion.5
  431.6 5.7 psum.72
  437.2 1.8 multiply_reduce_fusion.4
  439.1 6.6 psum.73
  445.9 5.8 all_gather.28
  452.8 23.3 %fusion.24 = f32[16,16,512]{2,0,1:T(8,128)S(1)} fusion(f32[16,512,512]{2,0,1:T(8,128)} %copy-done, f32[16,16,512]{2,1,0:T(8,128)S(1)} %convolution_bitcast_fusion.1), kind=kOutput, calls=%fused_computation.24 | convolution fusion | flops 805306368 | bytes 17825792 | tf_op jit(solution)/shard_map/rsa,sab->rsb/dot_general | solution.py:67
  476.8 1.1 copy.74
  478.3 30.0 %fusion.21 = f32[16,16,512]{2,0,1:T(8,128)S(1)} fusion(f32[16,512,512]{2,0,1:T(8,128)} %copy-done, f32[16,16,512]{2,1,0:T(8,128)S(1)} %convolution_bitcast_fusion.4), kind=kOutput, calls=%fused_computation.23 | convolution fusion | flops 805306368 | bytes 17825792 | tf_op jit(solution)/shard_map/rsb,sab->rsa/dot_general | solution.py:66
  508.3 0.9 convolution_convert_fusion.2
  509.2 1.1 copy.72
  511.1 70.2 %all-reduce.6.cloned.1.call-done = bf16[16,16384]{1,0:T(8,128)(2,1)} async-done(((bf16[16,16384]{1,0:T(8,128)(2,1)}), bf16[16,16384]{1,0:T(8,128)(2,1)}) %all-reduce.6.cloned.1.call-update) | async-done | bytes 524304 | tf_op jit(solution)/shard_map/psum | solution.py:154
  581.3 41.7 %all-gather.9.cloned.1.call-done = f32[16,16384]{1,0:T(8,128)} async-done(((f32[16,2048]{1,0:T(8,128)}), f32[16,16384]{1,0:T(8,128)}) %all-gather.9.cloned.1.call-update) | async-done | bytes 1048592 | tf_op jit(solution)/shard_map/all_gather | solution.py:156
  622.9 1.8 multiply_reduce_fusion.3
  624.8 5.7 psum.75
  630.4 1.9 multiply_reduce_fusion.2
  632.3 6.6 psum.76
  639.1 5.8 all_gather.30
  646.1 23.4 %fusion.30 = f32[16,16,512]{2,0,1:T(8,128)S(1)} fusion(f32[16,512,512]{2,0,1:T(8,128)} %copy-done, f32[16,16,512]{2,1,0:T(8,128)S(1)} %convolution_bitcast_fusion), kind=kOutput, calls=%fused_computation.26 | convolution fusion | flops 805306368 | bytes 17825792 | tf_op jit(solution)/shard_map/rsa,sab->rsb/dot_general | solution.py:67
  670.2 1.1 copy.78
  671.7 29.7 %fusion.27 = f32[16,16,512]{2,0,1:T(8,128)S(1)} fusion(f32[16,512,512]{2,0,1:T(8,128)} %copy-done, f32[16,16,512]{2,1,0:T(8,128)S(1)} %convolution_bitcast_fusion.3), kind=kOutput, calls=%fused_computation.25 | convolution fusion | flops 805306368 | bytes 17825792 | tf_op jit(solution)/shard_map/rsb,sab->rsa/dot_general | solution.py:66
  701.4 0.9 convolution_convert_fusion.1
  702.3 1.1 copy.76
  704.1 70.4 %all-reduce.8.cloned.1.call-done = bf16[16,16384]{1,0:T(8,128)(2,1)} async-done(((bf16[16,16384]{1,0:T(8,128)(2,1)}), bf16[16,16384]{1,0:T(8,128)(2,1)}) %all-reduce.8.cloned.1.call-update) | async-done | bytes 524304 | tf_op jit(solution)/shard_map/psum | solution.py:154
  774.5 41.5 %all-gather.11.cloned.1.call-done = f32[16,16384]{1,0:T(8,128)} async-done(((f32[16,2048]{1,0:T(8,128)}), f32[16,16384]{1,0:T(8,128)}) %all-gather.11.cloned.1.call-update) | async-done | bytes 1048592 | tf_op jit(solution)/shard_map/all_gather | solution.py:156
  816.0 1.8 multiply_reduce_fusion.1
  817.8 5.7 psum.78
  823.5 3.5 multiply_subtract_fusion.1
  827.0 6.6 psum.79
  833.7 1.8 multiply_add_fusion.1
  (82 shorter events, 13.0 us)
Async XLA Ops:
  8.3 29.6 %all-to-all-start = ((s32[8,1,2]{2,1,0:T(1,128)}), s32[8,1,2]{2,1,0:T(1,128)S(1)}, u32[]{:S(2)}, u32[]{:S(2)}) async-start(s32[8,1,2]{2,1,0:T(1,128)} %bitcast.2), calls=%async_computation | async-start | bytes 8192 | tf_op jit(solution)/shard_map/all_to_all | solution.py:135
  37.9 7.0 copy-start.4
  37.9 217.7 %all-to-all-start.1 = ((bf16[8,2,512,512]{3,2,1,0:T(8,128)(2,1)}), bf16[8,2,512,512]{3,2,1,0:T(8,128)(2,1)}, u32[]{:S(2)}, u32[]{:S(2)}) async-start(bf16[8,2,512,512]{3,2,1,0:T(8,128)(2,1)} %select_select_fusion), calls=%async_computation.1 | async-start | bytes 16777216 | tf_op jit(solution)/shard_map/all_to_all | solution.py:128
  44.1 195.8 %all-gather.5.cloned.1.call-start = ((), (), s32[]{:S(2)}) async-start(), calls=%async_computation.5 | async-start | bytes 1179648 | tf_op jit(solution)/shard_map/all_gather | solution.py:140
  44.8 273.3 %reduce-scatter.4.cloned.1.call-start = ((), (), s32[]{:S(2)}) async-start(), calls=%async_computation.7 | async-start | bytes 655360 | tf_op jit(solution)/shard_map/reduce_scatter | solution.py:155
  264.8 19.0 %copy-start = (f32[16,512,512]{2,0,1:T(8,128)}, f32[16,512,512]{2,0,1:T(8,128)S(1)}, u32[]{:S(2)}) copy-start(f32[16,512,512]{2,0,1:T(8,128)S(1)} %fusion.12) | copy-start | bytes 50331652
  285.7 102.6 %all-reduce.4.cloned.1.call-start = ((), (), s32[]{:S(2)}) async-start(), calls=%async_computation.6 | async-start | bytes 1048576 | tf_op jit(solution)/shard_map/psum | solution.py:154
  286.0 32.8 %copy-start.3 = (f32[2048]{0:T(1024)S(1)}, f32[2048]{0:T(1024)}, u32[]{:S(2)}) copy-start(f32[2048]{0:T(1024)} %param.11) | copy-start | bytes 24580
  286.0 143.8 %copy-start.1 = (f32[16,16384]{1,0:T(8,128)S(1)}, f32[16,16384]{1,0:T(8,128)}, u32[]{:S(2)}) copy-start(f32[16,16384]{1,0:T(8,128)} %all-gather.5.cloned.1.call-done) | copy-start | bytes 3145732
  318.1 111.7 %all-gather.7.cloned.1.call-start = ((), (), s32[]{:S(2)}) async-start(), calls=%async_computation.8 | async-start | bytes 1179648 | tf_op jit(solution)/shard_map/all_gather | solution.py:156
  318.7 191.7 %reduce-scatter.6.cloned.1.call-start = ((), (), s32[]{:S(2)}) async-start(), calls=%async_computation.10 | async-start | bytes 655360 | tf_op jit(solution)/shard_map/reduce_scatter | solution.py:155
  478.0 103.3 %all-reduce.6.cloned.1.call-start = ((), (), s32[]{:S(2)}) async-start(), calls=%async_computation.9 | async-start | bytes 1048576 | tf_op jit(solution)/shard_map/psum | solution.py:154
  510.3 112.6 %all-gather.9.cloned.1.call-start = ((), (), s32[]{:S(2)}) async-start(), calls=%async_computation.11 | async-start | bytes 1179648 | tf_op jit(solution)/shard_map/all_gather | solution.py:156
  511.1 192.5 %reduce-scatter.8.cloned.1.call-start = ((), (), s32[]{:S(2)}) async-start(), calls=%async_computation.13 | async-start | bytes 655360 | tf_op jit(solution)/shard_map/reduce_scatter | solution.py:155
  639.1 5.9 copy-start.2
  671.4 103.1 %all-reduce.8.cloned.1.call-start = ((), (), s32[]{:S(2)}) async-start(), calls=%async_computation.12 | async-start | bytes 1048576 | tf_op jit(solution)/shard_map/psum | solution.py:154
  703.5 112.5 %all-gather.11.cloned.1.call-start = ((), (), s32[]{:S(2)}) async-start(), calls=%async_computation.14 | async-start | bytes 1179648 | tf_op jit(solution)/shard_map/all_gather | solution.py:156
Sparse Core Ops, SparseCore 0:
  47.1 192.7 all-gather.4
  285.8 18.9 reduce-scatter.3
  318.2 70.0 all-reduce.3
  390.3 39.4 all-gather.6
  478.1 19.7 reduce-scatter.5
  510.4 70.8 all-reduce.5
  583.5 39.4 all-gather.8
  671.5 19.7 reduce-scatter.7
  703.6 70.8 all-reduce.7
  776.5 39.4 all-gather.10
where the time goes:
time: 851 us; the launch traced here: 843 us
  waiting for transfers between devices  500 us (59%)
  matrix products  179 us (21%)
  blocking collectives  90.6 us (11%)
  other arithmetic  27 us (3%)
  local copies, waits for them, and re-layouts  17.1 us (2%)
  between operations  14.1 us (2%)
  starting transfers between devices  13.9 us (2%)
    all_gather x1, waiting for transfers between devices, body(): lax.all_gather(right_sides, 'col', axis=1, tiled=True)  194 us
    psum x3, waiting for transfers between devices, operate_bands(): lax.psum(rows_part.astype(jnp.bfloat16), 'col').astype(jnp.float32)  179 us
    all_gather x3, waiting for transfers between devices, operate_bands(): from_columns = lax.all_gather(own_columns, 'col', axis=1, tiled=True)  125 us
    dot_general x3, matrix products, local_products(): jnp.einsum('rsb,sab->rsa', at_columns, matrix, precision=highest)  89.8 us
    dot_general x3, matrix products, local_products(): jnp.einsum('rsa,sab->rsb', at_rows, matrix, precision=highest)  65.7 us
    psum x7, blocking collectives, band_totals(): return lax.psum(partial_value, 'row')  42.4 us
    all_gather x1, blocking collectives, body(): lax.all_gather(diagonal, 'col', axis=0, tiled=True)  30.6 us
    all_gather x3, blocking collectives, operate_bands(): lax.all_gather(own_block.astype(jnp.bfloat16), 'row', axis=1, tiled=True)  17.5 us
  transfers between devices with their start and end apart: 12, of which 7 were waited for; matrix products, arithmetic and copies ran while one was open for 15% of the time, Pallas kernels for 0%

commit v1 on v0

v1 whole, which is shorter than its diff:
```python
import jax
import jax.numpy as jnp
from jax import lax
from jax.sharding import PartitionSpec as P

ITERS = 3


def block_places(bundle_tile_slot, tile_pos, blk_dev):
    row_count, col_count = lax.axis_size("row"), lax.axis_size("col")
    cap = tile_pos.shape[-1]
    band_pos = lax.all_gather(tile_pos.reshape(-1), "col", axis=0, tiled=True)
    owner = bundle_tile_slot // cap % col_count
    position = jnp.take(band_pos, bundle_tile_slot % (cap * col_count))
    span = row_count * blk_dev
    local = position % span
    rows = lax.axis_index("row") * col_count * blk_dev + position // span
    cols = (local // blk_dev * col_count + owner) * blk_dev + local % blk_dev
    return rows, cols


def body(left_derivatives, right_derivatives, bundle_tile_slot, tile_pos, right_sides, diagonal):
    width = left_derivatives.shape[2]
    nrhs, own = right_sides.shape
    blk = own // width
    blocks = blk * lax.axis_size("row") * lax.axis_size("col")
    axes = ("row", "col")
    b = right_sides.reshape(nrhs, blk, width).transpose(1, 0, 2)
    diag = diagonal.reshape(blk, 1, width)
    gram = jnp.einsum(
        "nma,nmb->nab", left_derivatives, right_derivatives, preferred_element_type=jnp.float32
    ).astype(jnp.bfloat16)
    rows, cols = block_places(bundle_tile_slot, tile_pos, blk)
    targets = jnp.concatenate([rows, cols])
    scatter = (jnp.arange(blocks, dtype=jnp.int32)[:, None] == targets[None, :]).astype(jnp.bfloat16)

    def apply(x):
        everywhere = lax.all_gather(x.astype(jnp.bfloat16), axes, axis=0, tiled=True)
        at_rows = jnp.take(everywhere, rows, axis=0)
        at_cols = jnp.take(everywhere, cols, axis=0)
        row_terms = jnp.einsum("crb,cab->cra", at_cols, gram, preferred_element_type=jnp.float32)
        col_terms = jnp.einsum("cra,cab->crb", at_rows, gram, preferred_element_type=jnp.float32)
        terms = jnp.concatenate([row_terms, col_terms]).astype(jnp.bfloat16)
        total = jnp.einsum("kc,crp->krp", scatter, terms, preferred_element_type=jnp.float32)
        return lax.psum_scatter(
            total.astype(jnp.bfloat16), axes, scatter_dimension=0, tiled=True
        ).astype(jnp.float32)

    def sums(*terms):
        return lax.psum(jnp.stack([jnp.sum(t, axis=(0, 2)) for t in terms]), axes)

    def wide(s):
        return s[None, :, None]

    first = sums(b * b, diag * b * b)
    beta = jnp.sqrt(first[0])
    v = b / wide(beta)
    v_old = None
    sv = apply(b) / wide(beta)
    sigma = first[1] / first[0]
    zero = jnp.zeros((nrhs,), jnp.float32)
    delta_bar, eps, phi_bar = zero, zero, beta
    cs, sn = -jnp.ones((nrhs,), jnp.float32), zero
    w = w_old = out = jnp.zeros_like(b)
    for step in range(ITERS):
        y = diag * v + sv - wide(sigma) * v
        if step > 0:
            y = y - wide(beta) * v_old
        dots = sums(v * y, y * y, v * v)
        alpha = sigma * dots[2] + dots[0]
        shift = alpha - sigma
        beta_next = jnp.sqrt(
            jnp.maximum(dots[1] - 2 * shift * dots[0] + shift * shift * dots[2], 0.0)
        )
        eps_old = eps
        delta = cs * delta_bar + sn * alpha
        gamma_bar = sn * delta_bar - cs * alpha
        eps = sn * beta_next
        delta_bar = -cs * beta_next
        gamma = jnp.sqrt(gamma_bar * gamma_bar + beta_next * beta_next)
        cs = gamma_bar / gamma
        sn = beta_next / gamma
        phi = cs * phi_bar
        phi_bar = sn * phi_bar
        w_older, w_old = w_old, w
        w = (v - wide(eps_old) * w_older - wide(delta) * w_old) / wide(gamma)
        out = out + wide(phi) * w
        if step < ITERS - 1:
            z = apply(y)
            v_old = v
            sv = (z - wide(shift) * sv) / wide(beta_next)
            v = (y - wide(shift) * v) / wide(beta_next)
            beta, sigma = beta_next, alpha
    return out.transpose(1, 0, 2).reshape(nrhs, own)


def solution(mesh):
    placed = (
        P(("row", "col"), None, None),
        P(("row", "col"), None, None),
        P(("row", "col")),
        P("row", "col", None),
        P(None, ("row", "col")),
        P(("row", "col")),
    )
    return jax.shard_map(
        body, mesh=mesh, in_specs=placed, out_specs=P(None, ("row", "col")), check_vma=False
    )
```

time: 851 us -> 686 us (0.81)
  matrix products: 179 us -> 29 us
  blocking collectives: 90.6 us -> 166 us
  waiting for transfers between devices: 500 us -> 442 us
  other arithmetic: 27 us -> 7.47 us
  starting transfers between devices: 13.9 us -> 0.39 us
    reduce_scatter x3, waiting for transfers between devices: 0.05 us -> 299 us  [apply(): lax.psum_scatter(total.astype(jnp.bfloat16), axes, scatter_dimension=0, t...]
    psum x3 -> x0, waiting for transfers between devices: 179 us -> none  [operate_bands(): lax.psum(rows_part.astype(jnp.bfloat16), 'col').astype(jnp.float32)]
    all_gather x4 -> x3, waiting for transfers between devices: 318 us -> 143 us  [apply(): lax.all_gather(x.astype(jnp.bfloat16), axes, axis=0, tiled=True)]
    dot_general x19 -> x9, matrix products: 172 us -> 21.2 us  [the longest x3 10.1 us: apply(): jnp.einsum('crb,cab->cra', at_cols, gram, preferred_element_type=jnp.floa...]
    psum x7 -> x4, blocking collectives: 42.4 us -> 153 us  [sums(): return lax.psum(jnp.stack([jnp.sum(t, axis=(0, 2)) for t in terms]), axes)]
    all_gather x4 -> x1, blocking collectives: 48.2 us -> 13.1 us  [block_places(): band_pos = lax.all_gather(tile_pos.reshape(-1), 'col', axis=0, tiled=True)]
    all_to_all x2 -> x0, starting transfers between devices: 13.5 us -> none  [the longest x1 7.28 us: body(): lax.all_to_all(labels, 'col', split_axis=0, concat_axis=0, tiled=True)]
    reduce_sum x8 -> x4, other arithmetic: 10.9 us -> 0.72 us  [sums(): return lax.psum(jnp.stack([jnp.sum(t, axis=(0, 2)) for t in terms]), axes)]
  transfers between devices with their start and end apart: 12 -> 6, of which waited for: 7 -> 6; matrix products, arithmetic and copies ran while one was open for 15% -> 2% of each run, Pallas kernels for 0% -> 0%
where the time goes in v1:
time: 686 us; the launch traced here: 685 us
  waiting for transfers between devices  442 us (64%)
  blocking collectives  166 us (24%)
  matrix products  29 us (4%)
  local copies, waits for them, and re-layouts  25.4 us (4%)
  between operations  14.4 us (2%)
  other arithmetic  7.47 us (1%)
    reduce_scatter x3, waiting for transfers between devices, apply(): lax.psum_scatter(total.astype(jnp.bfloat16), axes, scatter_dimension=0, t...  299 us
    psum x4, blocking collectives, sums(): return lax.psum(jnp.stack([jnp.sum(t, axis=(0, 2)) for t in terms]), axes)  153 us
    all_gather x3, waiting for transfers between devices, apply(): lax.all_gather(x.astype(jnp.bfloat16), axes, axis=0, tiled=True)  143 us
  transfers between devices with their start and end apart: 6, of which 6 were waited for; matrix products, arithmetic and copies ran while one was open for 2% of the time, Pallas kernels for 0%

profile of v1, /device:TPU:0, one launch (start us, length us, event | category | flops | bytes accessed | tf_op | source)
XLA Modules:
  0.0 684.5 jit_solution(702508848343151249)
XLA Ops:
  6.5 1.5 copy.72
  8.2 1.3 dynamic-slice
  10.2 0.8 bitcast_dynamic-update-slice_fusion
  10.9 13.1 %all-reduce = s32[128]{0:T(128)S(1)} all-reduce(s32[128]{0:T(128)S(1)} %bitcast_dynamic-update-slice_fusion), channel_id=2, replica_groups=mesh['row'=4,'col'=8] {'col'}, use_global_device_ids=true, to_apply=%add | all-reduce | flops 128 | bytes 1024 | tf_op jit(solution)/shard_map/all_gather | solution.py:12
  24.0 0.7 compare_select_fusion.2
  24.7 0.6 gather_fusion
  25.3 0.7 compare_and_fusion.1
  26.0 0.7 compare_and_fusion
  26.7 0.1 pad_add_fusion
  26.8 7.8 %convolution_convert_fusion = bf16[8,512,512]{2,1,0:T(8,128)(2,1)} fusion(bf16[8,512,512]{2,1,0:T(8,128)(2,1)} %param.8, bf16[8,512,512]{2,1,0:T(8,128)(2,1)} %param.9), kind=kOutput, calls=%fused_computation.7 | convolution fusion | flops 2149580800 | bytes 12582912 | tf_op jit(solution)/shard_map/nma,nmb->nab/dot_general | solution.py:30
  34.6 34.9 %all-gather.5.cloned.1.call-done = bf16[128,16,512]{2,1,0:T(8,128)(2,1)} async-done(((bf16[4,16,512]{2,1,0:T(8,128)(2,1)}), bf16[128,16,512]{2,1,0:T(8,128)(2,1)}) %all-gather.5.cloned.1.call-update) | async-done | bytes 2097168 | tf_op jit(solution)/shard_map/all_gather | solution.py:38
  69.5 2.1 gather_fusion.2
  71.6 2.9 convolution_convert_fusion.8
  74.5 2.2 gather_fusion.1
  76.7 3.4 convolution_convert_fusion.9
  80.1 0.8 convolution_convert_fusion.3
  80.9 2.5 copy.38
  83.5 0.1 fusion.7
  83.7 38.7 %psum.28 = f32[2,16]{1,0:T(2,128)S(1)} all-reduce(f32[2,16]{1,0:T(2,128)S(1)} %pad_maximum_fusion.6), channel_id=1, replica_groups=mesh['row'=4,'col'=8] {'row','col'}, use_global_device_ids=true, to_apply=%region_2.3 | all-reduce | flops 32 | bytes 256 | tf_op jit(solution)/shard_map/psum | solution.py:50
  122.4 99.7 %reduce-scatter.4.cloned.1.call-done = bf16[4,16,512]{2,1,0:T(8,128)(2,1)} async-done(((bf16[128,16,512]{2,1,0:T(8,128)(2,1)}), bf16[4,16,512]{2,1,0:T(8,128)(2,1)}) %reduce-scatter.4.cloned.1.call-update) | async-done | bytes 65552 | tf_op jit(solution)/shard_map/reduce_scatter | solution.py:45
  222.1 1.6 fusion.58
  223.7 54.3 %all-gather.7.cloned.1.call-done = bf16[128,16,512]{2,1,0:T(8,128)(2,1)} async-done(((bf16[4,16,512]{2,1,0:T(8,128)(2,1)}), bf16[128,16,512]{2,1,0:T(8,128)(2,1)}) %all-gather.7.cloned.1.call-update) | async-done | bytes 2097168 | tf_op jit(solution)/shard_map/all_gather | solution.py:38
  278.0 2.1 gather_fusion.4
  280.2 2.9 convolution_convert_fusion.6
  283.1 2.2 gather_fusion.3
  285.2 3.4 convolution_convert_fusion.7
  288.7 0.8 convolution_convert_fusion.2
  289.5 2.5 copy.40
  292.0 0.2 multiply_reduce_fusion.8
  292.3 38.7 %psum.29 = f32[3,16]{1,0:T(4,128)S(1)} all-reduce(f32[3,16]{1,0:T(4,128)S(1)} %pad_maximum_fusion.3), channel_id=1, replica_groups=mesh['row'=4,'col'=8] {'row','col'}, use_global_device_ids=true, to_apply=%region_7.9 | all-reduce | flops 48 | bytes 384 | tf_op jit(solution)/shard_map/psum | solution.py:50
  331.0 99.4 %reduce-scatter.6.cloned.1.call-done = bf16[4,16,512]{2,1,0:T(8,128)(2,1)} async-done(((bf16[128,16,512]{2,1,0:T(8,128)(2,1)}), bf16[4,16,512]{2,1,0:T(8,128)(2,1)}) %reduce-scatter.6.cloned.1.call-update) | async-done | bytes 65552 | tf_op jit(solution)/shard_map/reduce_scatter | solution.py:45
  430.4 1.6 fusion.57
  432.1 0.2 reduce-scatter.8.cloned.1.call-start
  432.3 53.9 %all-gather.9.cloned.1.call-done = bf16[128,16,512]{2,1,0:T(8,128)(2,1)} async-done(((bf16[4,16,512]{2,1,0:T(8,128)(2,1)}), bf16[128,16,512]{2,1,0:T(8,128)(2,1)}) %all-gather.9.cloned.1.call-update) | async-done | bytes 2097168 | tf_op jit(solution)/shard_map/all_gather | solution.py:38
  486.3 2.1 gather_fusion.5
  488.4 3.4 convolution_convert_fusion.5
  491.8 2.2 gather_fusion.6
  494.0 2.9 convolution_convert_fusion.4
  496.9 0.8 convolution_convert_fusion.1
  497.7 2.5 copy.42
  500.3 0.2 multiply_reduce_fusion.5
  500.4 38.8 %psum.30 = f32[3,16]{1,0:T(4,128)S(1)} all-reduce(f32[3,16]{1,0:T(4,128)S(1)} %pad_maximum_fusion.4), channel_id=1, replica_groups=mesh['row'=4,'col'=8] {'row','col'}, use_global_device_ids=true, to_apply=%region_12.14 | all-reduce | flops 48 | bytes 384 | tf_op jit(solution)/shard_map/psum | solution.py:50
  539.3 99.5 %reduce-scatter.8.cloned.1.call-done = bf16[4,16,512]{2,1,0:T(8,128)(2,1)} async-done(((bf16[128,16,512]{2,1,0:T(8,128)(2,1)}), bf16[4,16,512]{2,1,0:T(8,128)(2,1)}) %reduce-scatter.8.cloned.1.call-update) | async-done | bytes 65552 | tf_op jit(solution)/shard_map/reduce_scatter | solution.py:45
  638.8 1.0 multiply_subtract_fusion
  639.8 0.2 multiply_reduce_fusion.2
  639.9 36.9 %psum.31 = f32[3,16]{1,0:T(4,128)S(1)} all-reduce(f32[3,16]{1,0:T(4,128)S(1)} %pad_maximum_fusion.5), channel_id=1, replica_groups=mesh['row'=4,'col'=8] {'row','col'}, use_global_device_ids=true, to_apply=%region_17.19 | all-reduce | flops 48 | bytes 384 | tf_op jit(solution)/shard_map/psum | solution.py:50
  676.9 0.2 add_bitcast_fusion
  677.0 0.7 copy.46
  (41 shorter events, 0.6 us)
Async XLA Ops:
  6.5 62.9 %all-gather.5.cloned.1.call-start = ((), (), s32[]{:S(2)}) async-start(), calls=%async_computation.3 | async-start | bytes 2162688 | tf_op jit(solution)/shard_map/all_gather | solution.py:38
  8.1 214.0 %reduce-scatter.4.cloned.1.call-start = ((), (), s32[]{:S(2)}) async-start(), calls=%async_computation.4 | async-start | bytes 2162688 | tf_op jit(solution)/shard_map/reduce_scatter | solution.py:45
  80.1 3.4 copy-start.3
  80.1 3.4 copy-start
  83.4 194.6 %all-gather.7.cloned.1.call-start = ((), (), s32[]{:S(2)}) async-start(), calls=%async_computation.5 | async-start | bytes 2162688 | tf_op jit(solution)/shard_map/all_gather | solution.py:38
  223.7 206.8 %reduce-scatter.6.cloned.1.call-start = ((), (), s32[]{:S(2)}) async-start(), calls=%async_computation.6 | async-start | bytes 2162688 | tf_op jit(solution)/shard_map/reduce_scatter | solution.py:45
  288.7 141.8 %copy-start.1 = (bf16[4,16,512]{2,1,0:T(8,128)(2,1)S(1)}, bf16[4,16,512]{2,1,0:T(8,128)(2,1)}, u32[]{:S(2)}) copy-start(bf16[4,16,512]{2,1,0:T(8,128)(2,1)} %reduce-scatter.4.cloned.1.call-done) | copy-start | bytes 196612
  292.0 194.3 %all-gather.9.cloned.1.call-start = ((), (), s32[]{:S(2)}) async-start(), calls=%async_computation.7 | async-start | bytes 2162688 | tf_op jit(solution)/shard_map/all_gather | solution.py:38
  432.1 206.7 %reduce-scatter.8.cloned.1.call-start = ((), (), s32[]{:S(2)}) async-start(), calls=%async_computation.8 | async-start | bytes 2162688 | tf_op jit(solution)/shard_map/reduce_scatter | solution.py:45
  496.9 141.9 %copy-start.2 = (bf16[4,16,512]{2,1,0:T(8,128)(2,1)S(1)}, bf16[4,16,512]{2,1,0:T(8,128)(2,1)}, u32[]{:S(2)}) copy-start(bf16[4,16,512]{2,1,0:T(8,128)(2,1)} %reduce-scatter.6.cloned.1.call-done) | copy-start | bytes 196612
Sparse Core Ops, SparseCore 0:
  10.3 59.1 all-gather.4
  83.6 138.4 reduce-scatter.3
  225.1 52.9 all-gather.6
  292.1 138.2 reduce-scatter.5
  433.3 52.9 all-gather.8
  500.4 138.3 reduce-scatter.7

commit v2 on v1

v2 whole, which is shorter than its diff:
```python
import functools

import jax
import jax.numpy as jnp
from jax import lax
from jax.experimental import pallas as pl
from jax.experimental.pallas import tpu as pltpu
from jax.sharding import PartitionSpec as P

ITERS = 3
CORES = 2
MESH = pl.DeviceIdType.MESH


class Layout:
    def __init__(self, rows, cols, blk):
        self.Y, self.C = rows // CORES, CORES
        x = 1
        while 4 * x * x <= cols:
            x *= 2
        self.X, self.Z = x, cols // x
        self.devices = rows * cols
        self.hb = blk // 2
        self.size = {"z": self.Z, "x": self.X, "y": self.Y, "core": self.C}
        self.orders = (("z", "x", "y", "core"), ("z", "y", "x", "core"))
        self.strides = []
        for order in self.orders:
            strides, run = [], 1
            for axis in order:
                strides.append(run)
                run *= self.size[axis]
            self.strides.append(strides)

    def coords(self, row, col):
        return {"z": col // self.X, "x": col % self.X, "y": row // CORES, "core": row % CORES}

    def device(self, c):
        return (c["y"] * CORES + c["core"], c["z"] * self.X + c["x"])

    def base(self, half, c, level):
        order, strides = self.orders[half], self.strides[half]
        return sum(c[order[l]] * strides[l] for l in range(level, 4))

    def block(self, row, col, m):
        c = self.coords(row, col)
        half = m // self.hb
        at = jnp.where(half == 0, self.base(0, c, 0), self.base(1, c, 0))
        return (half * self.devices + at) * self.hb + m % self.hb


def kernel(
    lay, nb, width, nrhs, blk,
    pick_ref, prev_ref, last_ref, left_hbm, right_hbm, b_ref, d_ref, out_ref,
    lbuf, rbuf, gram, xall, part, r0, r1, r2, r3, acc, dots,
    v, v_old, sv, y, w, w_old, z,
    in_sem, ag_send, ag_recv, rs_send, rs_recv,
):
    row, col = lax.axis_index("row"), lax.axis_index("col")
    me = lay.coords(row, col)
    hb = lay.hb
    half_blocks = lay.devices * hb
    recv_bufs = (r0, r1, r2, r3)

    def peer(axis, offset):
        other = dict(me)
        other[axis] = lax.rem(me[axis] + offset, lay.size[axis])
        return other

    for i in range(nb):
        pltpu.make_async_copy(left_hbm.at[i], lbuf.at[i], in_sem.at[0, i]).start()
        pltpu.make_async_copy(right_hbm.at[i], rbuf.at[i], in_sem.at[1, i]).start()

    barrier = pltpu.get_barrier_semaphore()
    greeted = 0
    for axis in ("z", "x", "y", "core"):
        for o in range(1, lay.size[axis]):
            pl.semaphore_signal(
                barrier, inc=1, device_id=lay.device(peer(axis, o)), device_id_type=MESH
            )
            greeted += 1
    pl.semaphore_wait(barrier, greeted)

    dot_axes = ("z", "x", "y", "core")
    lane = lax.broadcasted_iota(jnp.int32, (nrhs, 128), 1)

    def put_dots(*values):
        tile = jnp.zeros((nrhs, 128), jnp.float32)
        for j, value in enumerate(values):
            tile = jnp.where(lane == j, jnp.sum(value, axis=1, keepdims=True), tile)
        dots[0, me["z"]] = tile

    def start_dots(level):
        copies = []
        axis = dot_axes[level]
        for o in range(1, lay.size[axis]):
            src = dots.at[level, me[axis]]
            copy = pltpu.make_async_remote_copy(
                src_ref=src, dst_ref=src,
                send_sem=ag_send.at[2, level, o], recv_sem=ag_recv.at[2, level, o],
                device_id=lay.device(peer(axis, o)), device_id_type=MESH,
            )
            copy.start()
            copies.append(copy)
        return copies

    def sum_dots(level):
        total = dots[level, 0]
        for s in range(1, lay.size[dot_axes[level]]):
            total = total + dots[level, s]
        if level < 3:
            dots[level + 1, me[dot_axes[level + 1]]] = total
        return total

    def pick_dot(total, j):
        return jnp.sum(jnp.where(lane == j, total, 0.0), axis=1, keepdims=True)

    def gather(x_ref, hook=None):
        for m in range(blk):
            h = m // hb
            xall[h * half_blocks + lay.base(h, me, 0) * hb + m % hb] = x_ref[
                :, m * width:(m + 1) * width
            ].astype(jnp.bfloat16)
        total = None
        for level in range(4):
            copies = start_dots(level)
            for h in range(2):
                axis = lay.orders[h][level]
                run = lay.strides[h][level] * hb
                src = xall.at[pl.ds(h * half_blocks + lay.base(h, me, level) * hb, run)]
                for o in range(1, lay.size[axis]):
                    copy = pltpu.make_async_remote_copy(
                        src_ref=src, dst_ref=src,
                        send_sem=ag_send.at[h, level, o], recv_sem=ag_recv.at[h, level, o],
                        device_id=lay.device(peer(axis, o)), device_id_type=MESH,
                    )
                    copy.start()
                    copies.append(copy)
            if hook is not None:
                hook(level)
            for copy in copies:
                copy.wait()
            total = sum_dots(level)
        return total

    def reduce_dots():
        total = None
        for level in range(4):
            for copy in start_dots(level):
                copy.wait()
            total = sum_dots(level)
        return total

    def products():
        acc[2 * nb] = jnp.zeros((nrhs, width), jnp.float32)

        def one(i, carry):
            g = gram[i]
            x_row = xall[pick_ref[2 * i]]
            x_col = xall[pick_ref[2 * i + 1]]
            row_term = lax.dot_general(
                x_col, g, (((1,), (1,)), ((), ())), preferred_element_type=jnp.float32
            )
            col_term = jnp.dot(x_row, g, preferred_element_type=jnp.float32)
            acc[2 * i] = row_term + acc[prev_ref[2 * i]]
            acc[2 * i + 1] = col_term + acc[prev_ref[2 * i + 1]]
            return carry

        lax.fori_loop(0, nb, one, 0)

        def spread(k, carry):
            for u in range(4):
                part[4 * k + u] = acc[last_ref[4 * k + u]].astype(jnp.bfloat16)
            return carry

        lax.fori_loop(0, 2 * half_blocks // 4, spread, 0)

    def scatter_sum():
        for level in (3, 2, 1, 0):
            copies = []
            for h in range(2):
                axis = lay.orders[h][level]
                run = lay.strides[h][level] * hb
                for o in range(1, lay.size[axis]):
                    other = peer(axis, o)
                    at = dict(me)
                    at[axis] = other[axis]
                    copy = pltpu.make_async_remote_copy(
                        src_ref=part.at[pl.ds(h * half_blocks + lay.base(h, at, level) * hb, run)],
                        dst_ref=recv_bufs[level].at[h, o - 1, pl.ds(0, run)],
                        send_sem=rs_send.at[h, level, o], recv_sem=rs_recv.at[h, level, o],
                        device_id=lay.device(other), device_id_type=MESH,
                    )
                    copy.start()
                    copies.append(copy)
            for copy in copies:
                copy.wait()
            for h in range(2):
                axis = lay.orders[h][level]
                run = lay.strides[h][level] * hb
                start = h * half_blocks + lay.base(h, me, level) * hb

                def total(i):
                    value = part[start + i].astype(jnp.float32)
                    for o in range(1, lay.size[axis]):
                        value = value + recv_bufs[level][h, o - 1, i].astype(jnp.float32)
                    return value

                if level == 0:
                    for i in range(hb):
                        m = h * hb + i
                        z[:, m * width:(m + 1) * width] = total(i)
                else:

                    def add(i, carry):
                        for u in range(2):
                            part[start + 2 * i + u] = total(2 * i + u).astype(jnp.bfloat16)
                        return carry

                    lax.fori_loop(0, run // 2, add, 0)

    def make_grams(level):
        def one(i, carry):
            pltpu.make_async_copy(left_hbm.at[i], lbuf.at[i], in_sem.at[0, i]).wait()
            pltpu.make_async_copy(right_hbm.at[i], rbuf.at[i], in_sem.at[1, i]).wait()
            gram[i] = lax.dot_general(
                lbuf[i], rbuf[i], (((0,), (0,)), ((), ())), preferred_element_type=jnp.float32
            ).astype(jnp.bfloat16)
            return carry

        lax.fori_loop(level * nb // 4, (level + 1) * nb // 4, one, 0)

    b = b_ref[...]
    put_dots(b * b, d_ref[...] * b * b)
    total = gather(b_ref, make_grams)
    first = pick_dot(total, 0)
    beta = jnp.sqrt(first)
    sigma = pick_dot(total, 1) / first
    products()
    scatter_sum()
    v[...] = b_ref[...] / beta
    sv[...] = z[...] / beta
    zero = jnp.zeros_like(beta)
    delta_bar, eps, phi_bar = zero, zero, beta
    cs, sn = -jnp.ones_like(beta), zero
    for step in range(ITERS):
        vv = v[...]
        value = d_ref[...] * vv + sv[...] - sigma * vv
        if step > 0:
            value = value - beta * v_old[...]
        y[...] = value
        put_dots(vv * value, value * value, vv * vv)
        total = gather(y) if step < ITERS - 1 else reduce_dots()
        vy, yy, ones = pick_dot(total, 0), pick_dot(total, 1), pick_dot(total, 2)
        alpha = sigma * ones + vy
        shift = alpha - sigma
        beta_next = jnp.sqrt(jnp.maximum(yy - 2 * shift * vy + shift * shift * ones, 0.0))
        eps_old = eps
        delta = cs * delta_bar + sn * alpha
        gamma_bar = sn * delta_bar - cs * alpha
        eps = sn * beta_next
        delta_bar = -cs * beta_next
        gamma = jnp.sqrt(gamma_bar * gamma_bar + beta_next * beta_next)
        cs = gamma_bar / gamma
        sn = beta_next / gamma
        phi = cs * phi_bar
        phi_bar = sn * phi_bar
        search = v[...]
        if step > 1:
            search = search - eps_old * w_old[...]
        if step > 0:
            search = search - delta * w[...]
            w_old[...] = w[...]
        search = search / gamma
        w[...] = search
        if step == 0:
            out_ref[...] = phi * search
            w_old[...] = jnp.zeros_like(search)
        else:
            out_ref[...] = out_ref[...] + phi * search
        if step < ITERS - 1:
            products()
            scatter_sum()
            v_old[...] = v[...]
            sv[...] = (z[...] - shift * sv[...]) / beta_next
            v[...] = (y[...] - shift * v[...]) / beta_next
            beta, sigma = beta_next, alpha


def body(rows, cols, left, right, bundle_tile_slot, tile_pos, right_sides, diagonal):
    nb, measures, width = left.shape
    nrhs, own = right_sides.shape
    blk = own // width
    lay = Layout(rows, cols, blk)
    cap = tile_pos.shape[-1]
    band_pos = lax.all_gather(tile_pos.reshape(-1), "col", axis=0, tiled=True)
    owner = bundle_tile_slot // cap % cols
    wanted = bundle_tile_slot % (cap * cols)
    hit = wanted[:, None] == jnp.arange(cap * cols, dtype=jnp.int32)[None, :]
    position = jnp.sum(jnp.where(hit, band_pos[None, :], 0), axis=1)
    span = rows * blk
    row_block, local = position // span, position % span
    at_row = lay.block(lax.axis_index("row"), row_block // blk, row_block % blk)
    at_col = lay.block(local // blk, owner, local % blk)
    target = jnp.stack([at_row, at_col], axis=1).reshape(-1)
    number = jnp.arange(2 * nb, dtype=jnp.int32)
    same = (target[:, None] == target[None, :]) & (number[None, :] < number[:, None])
    prev = jnp.max(jnp.where(same, number[None, :], -1), axis=1)
    prev = jnp.where(prev < 0, 2 * nb, prev)
    blocks = blk * rows * cols
    found = target[None, :] == jnp.arange(blocks, dtype=jnp.int32)[:, None]
    last = jnp.max(jnp.where(found, number[None, :], -1), axis=1)
    last = jnp.where(last < 0, 2 * nb, last)

    hb = lay.hb
    bf16, f32 = jnp.bfloat16, jnp.float32
    most = max(lay.size.values())

    def landing(level):
        peers = max(lay.size[order[level]] for order in lay.orders) - 1
        run = max(strides[level] for strides in lay.strides) * hb
        return pltpu.VMEM((2, max(peers, 1), run, nrhs, width), bf16)

    smem = pl.BlockSpec(memory_space=pltpu.SMEM)
    vmem = pl.BlockSpec(memory_space=pltpu.VMEM)
    hbm = pl.BlockSpec(memory_space=pl.ANY)
    state = pltpu.VMEM((nrhs, own), f32)
    return pl.pallas_call(
        functools.partial(kernel, lay, nb, width, nrhs, blk),
        out_shape=jax.ShapeDtypeStruct((nrhs, own), f32),
        in_specs=[smem, smem, smem, hbm, hbm, vmem, vmem],
        out_specs=vmem,
        scratch_shapes=[
            pltpu.VMEM((nb, measures, width), bf16),
            pltpu.VMEM((nb, measures, width), bf16),
            pltpu.VMEM((nb, width, width), bf16),
            pltpu.VMEM((blocks, nrhs, width), bf16),
            pltpu.VMEM((blocks, nrhs, width), bf16),
            landing(0), landing(1), landing(2), landing(3),
            pltpu.VMEM((2 * nb + 1, nrhs, width), f32),
            pltpu.VMEM((4, most, nrhs, 128), f32),
            state, state, state, state, state, state, state,
            pltpu.SemaphoreType.DMA((2, nb)),
            pltpu.SemaphoreType.DMA((3, 4, most)),
            pltpu.SemaphoreType.DMA((3, 4, most)),
            pltpu.SemaphoreType.DMA((2, 4, most)),
            pltpu.SemaphoreType.DMA((2, 4, most)),
        ],
        compiler_params=pltpu.CompilerParams(
            collective_id=0, has_side_effects=True, vmem_limit_bytes=60 * 1024 * 1024
        ),
    )(target, prev, last, left, right, right_sides, diagonal.reshape(1, own))


def solution(mesh):
    placed = (
        P(("row", "col"), None, None),
        P(("row", "col"), None, None),
        P(("row", "col")),
        P("row", "col", None),
        P(None, ("row", "col")),
        P(("row", "col")),
    )
    return jax.shard_map(
        functools.partial(body, mesh.shape["row"], mesh.shape["col"]),
        mesh=mesh, in_specs=placed, out_specs=P(None, ("row", "col")), check_vma=False,
    )
```

time: 686 us -> 171 us (0.25)
  waiting for transfers between devices: 442 us -> 0 us
  blocking collectives: 166 us -> 13.1 us
  Pallas kernels: 0 us -> 151 us
  matrix products: 29 us -> 0 us
  local copies, waits for them, and re-layouts: 25.4 us -> 3.71 us
  between operations: 14.4 us -> 0.67 us
    reduce_scatter x3 -> x0, waiting for transfers between devices: 299 us -> none  [apply(): lax.psum_scatter(total.astype(jnp.bfloat16), axes, scatter_dimension=0, t...]
    psum x4 -> x0, blocking collectives: 153 us -> none  [sums(): return lax.psum(jnp.stack([jnp.sum(t, axis=(0, 2)) for t in terms]), axes)]
    pallas_call x0 -> x1, Pallas kernels: none -> 151 us  [body(): pl.pallas_call(functools.partial(kernel, lay, nb, width, nrhs, blk), out_...]
    all_gather x3 -> x0, waiting for transfers between devices: 143 us -> none  [apply(): lax.all_gather(x.astype(jnp.bfloat16), axes, axis=0, tiled=True)]
    dot_general x10 -> x0, matrix products: 29 us -> none  [the longest x3 10.1 us: apply(): jnp.einsum('crb,cab->cra', at_cols, gram, preferred_element_type=jnp.floa...]
    gather x7 -> x0, local copies, waits for them, and re-layouts: 13.5 us -> none  [the longest x3 6.45 us: apply(): at_cols = jnp.take(everywhere, cols, axis=0)]
    all_gather x1 -> x0, blocking collectives: 13.1 us -> none  [block_places(): band_pos = lax.all_gather(tile_pos.reshape(-1), 'col', axis=0, tiled=True)]
    unnamed x0 -> x1, blocking collectives: none -> 13.1 us
  transfers between devices with their start and end apart: 6 -> 0, of which waited for: 6 -> 0; matrix products, arithmetic and copies ran while one was open for 2% -> 0% of each run, Pallas kernels for 0% -> 0%
where the time goes in v2:
time: 171 us
  Pallas kernels  151 us (88%)
  blocking collectives  13.1 us (8%)
  local copies, waits for them, and re-layouts  3.71 us (2%)
  other arithmetic  2.96 us (2%)
    pallas_call x1, Pallas kernels, body(): pl.pallas_call(functools.partial(kernel, lay, nb, width, nrhs, blk), out_...  151 us
    unnamed x1, blocking collectives  13.1 us
    unnamed x6, local copies, waits for them, and re-layouts  3.55 us

profile of v2, /device:TPU:0, one launch (start us, length us, event | category | flops | bytes accessed | tf_op | source)
XLA Modules:
  0.0 171.2 jit_solution(305925103978636258)
XLA Ops:
  0.0 1.2 dynamic-slice
  1.9 0.7 and_select_fusion.18
  2.6 0.7 bitcast_dynamic-update-slice_fusion
  3.3 13.1 %all-reduce = s32[128]{0:T(128)S(1)} all-reduce(s32[128]{0:T(128)S(1)} %bitcast_dynamic-update-slice_fusion), channel_id=2, replica_groups=mesh['row'=4,'col'=8] {'col'}, use_global_device_ids=true, to_apply=%add | all-reduce | flops 128 | bytes 1024
  16.4 0.2 select_reduce_fusion.2
  16.6 0.7 fusion.8
  17.3 0.1 copy.9
  17.4 0.1 reshape.297.pick_ref
  17.5 0.0 copy-start
  17.5 0.1 select_reduce_fusion
  17.6 0.6 compare_select_fusion.last_ref
  18.2 0.2 select_reduce_fusion.1
  18.3 0.5 compare_select_fusion.1.prev_ref
  18.8 0.0 copy-done
  18.9 150.8 %shard_map.64 = f32[16,2048]{1,0:T(8,128)} custom-call(s32[16]{0:T(128)} %copy-done, s32[16]{0:T(128)} %compare_select_fusion.1.prev_ref, s32[128]{0:T(128)} %compare_select_fusion.last_ref, bf16[8,512,512]{2,1,0:T(8,128)(2,1)} %left_hbm.1, bf16[8,512,512]{2,1,0:T(8,128)(2,1)} %right_hbm.1, f32[16,2048]{1,0:T(8,128)} %b_ref.1, f32[1,2048]{1,0:T(1,128)} %bitcast.16), custom_call_target="tpu_custom_call" | custom-call | tf_op jit(solution)/shard_map/pallas_call | solution.py:327
  169.6 1.6 copy.12
  (3 shorter events, 0.0 us)
Async XLA Ops:
  17.5 1.4 copy-start

commit v3 on v2

--- a/solution.py
+++ b/solution.py
@@ -22,14 +22,7 @@
         self.devices = rows * cols
         self.hb = blk // 2
         self.size = {"z": self.Z, "x": self.X, "y": self.Y, "core": self.C}
-        self.orders = (("z", "x", "y", "core"), ("z", "y", "x", "core"))
-        self.strides = []
-        for order in self.orders:
-            strides, run = [], 1
-            for axis in order:
-                strides.append(run)
-                run *= self.size[axis]
-            self.strides.append(strides)
+        self.orders = (("x", "y"), ("y", "x"))
 
     def coords(self, row, col):
         return {"z": col // self.X, "x": col % self.X, "y": row // CORES, "core": row % CORES}
@@ -37,29 +30,31 @@
     def device(self, c):
         return (c["y"] * CORES + c["core"], c["z"] * self.X + c["x"])
 
-    def base(self, half, c, level):
-        order, strides = self.orders[half], self.strides[half]
-        return sum(c[order[l]] * strides[l] for l in range(level, 4))
+    def chunk(self, half, c):
+        near, far = self.orders[half]
+        at = c["core"] * self.Z + c["z"]
+        return (at * self.size[far] + c[far]) * self.size[near] + c[near]
 
     def block(self, row, col, m):
         c = self.coords(row, col)
         half = m // self.hb
-        at = jnp.where(half == 0, self.base(0, c, 0), self.base(1, c, 0))
+        at = jnp.where(half == 0, self.chunk(0, c), self.chunk(1, c))
         return (half * self.devices + at) * self.hb + m % self.hb
 
 
 def kernel(
     lay, nb, width, nrhs, blk,
     pick_ref, prev_ref, last_ref, left_hbm, right_hbm, b_ref, d_ref, out_ref,
-    lbuf, rbuf, gram, xall, part, r0, r1, r2, r3, acc, dots,
+    lbuf, rbuf, gram, xall, part, r_z, r_near, r_far, r_core, acc, dots,
     v, v_old, sv, y, w, w_old, z,
-    in_sem, ag_send, ag_recv, rs_send, rs_recv,
+    in_sem, dot_send, dot_recv, *sems,
 ):
     row, col = lax.axis_index("row"), lax.axis_index("col")
     me = lay.coords(row, col)
     hb = lay.hb
     half_blocks = lay.devices * hb
-    recv_bufs = (r0, r1, r2, r3)
+    ag_z, ag_near, ag_far, ag_core = [sems[i:i + 2] for i in range(0, 8, 2)]
+    rs_z, rs_near, rs_far, rs_core = [sems[i:i + 2] for i in range(8, 16, 2)]
 
     def peer(axis, offset):
         other = dict(me)
@@ -96,7 +91,7 @@
             src = dots.at[level, me[axis]]
             copy = pltpu.make_async_remote_copy(
                 src_ref=src, dst_ref=src,
-                send_sem=ag_send.at[2, level, o], recv_sem=ag_recv.at[2, level, o],
+                send_sem=dot_send.at[level, o], recv_sem=dot_recv.at[level, o],
                 device_id=lay.device(peer(axis, o)), device_id_type=MESH,
             )
             copy.start()
@@ -114,33 +109,102 @@
     def pick_dot(total, j):
         return jnp.sum(jnp.where(lane == j, total, 0.0), axis=1, keepdims=True)
 
+    def place(h, oz=0, o1=0, o2=0, other_core=False):
+        near, far = lay.orders[h]
+        c = dict(me)
+        for axis, o in (("z", oz), (near, o1), (far, o2)):
+            if o:
+                c[axis] = lax.rem(me[axis] + o, lay.size[axis])
+        if other_core:
+            c["core"] = 1 - me["core"]
+        return h * half_blocks + lay.chunk(h, c) * hb
+
+    def group(h, oz, other_core=False):
+        c = dict(me, z=lax.rem(me["z"] + oz, lay.Z), x=0, y=0)
+        if other_core:
+            c["core"] = 1 - me["core"]
+        return h * half_blocks + lay.chunk(h, c) * hb
+
+    def send(src, dst, sems, index, other):
+        copy = pltpu.make_async_remote_copy(
+            src_ref=src, dst_ref=dst, send_sem=sems[0].at[index], recv_sem=sems[1].at[index],
+            device_id=lay.device(other), device_id_type=MESH,
+        )
+        copy.start()
+        return copy
+
+    spans = [[lay.size[axis] for axis in order] for order in lay.orders]
+    run = lay.X * lay.Y * hb
+    z_near_first = sorted(range(1, lay.Z), key=lambda o: (min(o, lay.Z - o), o))
+
     def gather(x_ref, hook=None):
         for m in range(blk):
             h = m // hb
-            xall[h * half_blocks + lay.base(h, me, 0) * hb + m % hb] = x_ref[
-                :, m * width:(m + 1) * width
-            ].astype(jnp.bfloat16)
-        total = None
-        for level in range(4):
-            copies = start_dots(level)
+            xall[place(h) + m % hb] = x_ref[:, m * width:(m + 1) * width].astype(jnp.bfloat16)
+        sent = []
+
+        def push(at, count, sems, index, other):
+            ref = xall.at[pl.ds(at, count)]
+            copy = send(ref, ref, sems, index, other)
+            sent.append(copy)
+            return copy
+
+        small = start_dots(0)
+        by_z, by_near, by_far, by_core = {}, {}, {}, []
+        for o in z_near_first:
             for h in range(2):
-                axis = lay.orders[h][level]
-                run = lay.strides[h][level] * hb
-                src = xall.at[pl.ds(h * half_blocks + lay.base(h, me, level) * hb, run)]
-                for o in range(1, lay.size[axis]):
-                    copy = pltpu.make_async_remote_copy(
-                        src_ref=src, dst_ref=src,
-                        send_sem=ag_send.at[h, level, o], recv_sem=ag_recv.at[h, level, o],
-                        device_id=lay.device(peer(axis, o)), device_id_type=MESH,
-                    )
-                    copy.start()
-                    copies.append(copy)
-            if hook is not None:
-                hook(level)
-            for copy in copies:
-                copy.wait()
-            total = sum_dots(level)
-        return total
+                by_z[h, o] = push(place(h), hb, ag_z, (h, o), peer("z", o))
+        order = [0] + z_near_first
+        slots = len(order)
+        for t in range(slots + 2):
+            if t < slots:
+                o = order[t]
+                oz = (lay.Z - o) % lay.Z
+                for h in range(2):
+                    if o:
+                        by_z[h, o].wait_recv()
+                    near, far = lay.orders[h]
+                    for o1 in range(1, spans[h][0]):
+                        by_near[h, oz, o1] = push(
+                            place(h, oz), hb, ag_near, (h, oz, o1), peer(near, o1)
+                        )
+                    for o2 in range(1, spans[h][1]):
+                        by_far[h, oz, 0, o2] = push(
+                            place(h, oz), hb, ag_far, (h, oz, 0, o2), peer(far, o2)
+                        )
+            if 1 <= t <= slots:
+                oz = (lay.Z - order[t - 1]) % lay.Z
+                for h in range(2):
+                    near, far = lay.orders[h]
+                    for o1 in range(1, spans[h][0]):
+                        by_near[h, oz, o1].wait_recv()
+                        back = spans[h][0] - o1
+                        for o2 in range(1, spans[h][1]):
+                            by_far[h, oz, back, o2] = push(
+                                place(h, oz, back), hb, ag_far, (h, oz, back, o2), peer(far, o2)
+                            )
+            if t >= 2:
+                oz = (lay.Z - order[t - 2]) % lay.Z
+                for h in range(2):
+                    for o1 in range(spans[h][0]):
+                        for o2 in range(1, spans[h][1]):
+                            by_far[h, oz, o1, o2].wait_recv()
+                    by_core.append(push(group(h, oz), run, ag_core, (h, oz), peer("core", 1)))
+            if hook is not None and t < 4:
+                hook(t)
+            level = {slots - 1: 0, slots: 1, slots + 1: 2}.get(t)
+            if level is not None:
+                for copy in small:
+                    copy.wait()
+                sum_dots(level)
+                small = start_dots(level + 1)
+        for copy in by_core:
+            copy.wait_recv()
+        for copy in sent:
+            copy.wait_send()
+        for copy in small:
+            copy.wait()
+        return sum_dots(3)
 
     def reduce_dots():
         total = None
@@ -167,56 +231,91 @@
 
         lax.fori_loop(0, nb, one, 0)
 
-        def spread(k, carry):
-            for u in range(4):
-                part[4 * k + u] = acc[last_ref[4 * k + u]].astype(jnp.bfloat16)
-            return carry
-
-        lax.fori_loop(0, 2 * half_blocks // 4, spread, 0)
-
     def scatter_sum():
-        for level in (3, 2, 1, 0):
-            copies = []
+        sent = []
+        z_far_first = z_near_first[::-1] + [0]
+        by_core, by_far, by_near, by_z = {}, {}, {}, {}
+        for oz in z_far_first:
             for h in range(2):
-                axis = lay.orders[h][level]
-                run = lay.strides[h][level] * hb
-                for o in range(1, lay.size[axis]):
-                    other = peer(axis, o)
-                    at = dict(me)
-                    at[axis] = other[axis]
-                    copy = pltpu.make_async_remote_copy(
-                        src_ref=part.at[pl.ds(h * half_blocks + lay.base(h, at, level) * hb, run)],
-                        dst_ref=recv_bufs[level].at[h, o - 1, pl.ds(0, run)],
-                        send_sem=rs_send.at[h, level, o], recv_sem=rs_recv.at[h, level, o],
-                        device_id=lay.device(other), device_id_type=MESH,
-                    )
-                    copy.start()
-                    copies.append(copy)
-            for copy in copies:
-                copy.wait()
-            for h in range(2):
-                axis = lay.orders[h][level]
-                run = lay.strides[h][level] * hb
-                start = h * half_blocks + lay.base(h, me, level) * hb
-
-                def total(i):
-                    value = part[start + i].astype(jnp.float32)
-                    for o in range(1, lay.size[axis]):
-                        value = value + recv_bufs[level][h, o - 1, i].astype(jnp.float32)
-                    return value
-
-                if level == 0:
-                    for i in range(hb):
-                        m = h * hb + i
-                        z[:, m * width:(m + 1) * width] = total(i)
-                else:
-
-                    def add(i, carry):
-                        for u in range(2):
-                            part[start + 2 * i + u] = total(2 * i + u).astype(jnp.bfloat16)
-                        return carry
-
-                    lax.fori_loop(0, run // 2, add, 0)
+                at = group(h, oz, True)
+
+                def spread(i, carry):
+                    for u in range(2):
+                        k = at + 2 * i + u
+                        part[k] = acc[last_ref[k]].astype(jnp.bfloat16)
+                    return carry
+
+                lax.fori_loop(0, run // 2, spread, 0)
+                by_core[h, oz] = send(
+                    part.at[pl.ds(at, run)], r_core.at[h, oz], rs_core, (h, oz), peer("core", 1)
+                )
+                sent.append(by_core[h, oz])
+
+        def total(h, oz, o1, o2, i):
+            at = place(h, oz, o1, o2) + i
+            value = acc[last_ref[at]] + r_core[h, oz, at - group(h, oz)].astype(jnp.float32)
+            if o2 == 0:
+                for o in range(1, spans[h][1]):
+                    value = value + r_far[h, oz, o1, o - 1, i].astype(jnp.float32)
+                if o1 == 0:
+                    for o in range(1, spans[h][0]):
+                        value = value + r_near[h, oz, o - 1, i].astype(jnp.float32)
+                    if oz == 0:
+                        for o in range(1, lay.Z):
+                            value = value + r_z[h, o - 1, i].astype(jnp.float32)
+            return value
+
+        def forward(h, oz, o1, o2, dst, sems, index, other):
+            at = place(h, oz, o1, o2)
+            for i in range(hb):
+                part[at + i] = total(h, oz, o1, o2, i).astype(jnp.bfloat16)
+            copy = send(part.at[pl.ds(at, hb)], dst, sems, index, other)
+            sent.append(copy)
+            return copy
+
+        slots = len(z_far_first)
+        for t in range(slots + 2):
+            if t < slots:
+                oz = z_far_first[t]
+                for h in range(2):
+                    near, far = lay.orders[h]
+                    by_core[h, oz].wait_recv()
+                    for o1 in list(range(1, spans[h][0])) + [0]:
+                        for o2 in range(1, spans[h][1]):
+                            by_far[h, oz, o1, o2] = forward(
+                                h, oz, o1, o2, r_far.at[h, oz, o1, o2 - 1],
+                                rs_far, (h, oz, o1, o2), peer(far, o2),
+                            )
+            if 1 <= t <= slots:
+                oz = z_far_first[t - 1]
+                for h in range(2):
+                    near, far = lay.orders[h]
+                    for o1 in range(1, spans[h][0]):
+                        for o2 in range(1, spans[h][1]):
+                            by_far[h, oz, o1, o2].wait_recv()
+                        by_near[h, oz, o1] = forward(
+                            h, oz, o1, 0, r_near.at[h, oz, o1 - 1],
+                            rs_near, (h, oz, o1), peer(near, o1),
+                        )
+            if t >= 2:
+                oz = z_far_first[t - 2]
+                for h in range(2):
+                    for o2 in range(1, spans[h][1]):
+                        by_far[h, oz, 0, o2].wait_recv()
+                    for o1 in range(1, spans[h][0]):
+                        by_near[h, oz, o1].wait_recv()
+                    if oz:
+                        by_z[h, oz] = forward(
+                            h, oz, 0, 0, r_z.at[h, oz - 1], rs_z, (h, oz), peer("z", oz)
+                        )
+        for h in range(2):
+            for o in range(1, lay.Z):
+                by_z[h, o].wait_recv()
+            for i in range(hb):
+                m = h * hb + i
+                z[:, m * width:(m + 1) * width] = total(h, 0, 0, 0, i)
+        for copy in sent:
+            copy.wait_send()
 
     def make_grams(level):
         def one(i, carry):
@@ -315,11 +414,14 @@
     bf16, f32 = jnp.bfloat16, jnp.float32
     most = max(lay.size.values())
 
-    def landing(level):
-        peers = max(lay.size[order[level]] for order in lay.orders) - 1
-        run = max(strides[level] for strides in lay.strides) * hb
-        return pltpu.VMEM((2, max(peers, 1), run, nrhs, width), bf16)
-
+    wide = max(lay.X, lay.Y)
+    runs = lay.X * lay.Y * hb
+
+    def landing(*shape):
+        return pltpu.VMEM((2, *shape, nrhs, width), bf16)
+
+    counts = ((2, lay.Z), (2, lay.Z, wide), (2, lay.Z, wide, wide), (2, lay.Z))
+    sems = [pltpu.SemaphoreType.DMA(shape) for shape in counts for _ in range(2)] * 2
     smem = pl.BlockSpec(memory_space=pltpu.SMEM)
     vmem = pl.BlockSpec(memory_space=pltpu.VMEM)
     hbm = pl.BlockSpec(memory_space=pl.ANY)
@@ -335,15 +437,17 @@
             pltpu.VMEM((nb, width, width), bf16),
             pltpu.VMEM((blocks, nrhs, width), bf16),
             pltpu.VMEM((blocks, nrhs, width), bf16),
-            landing(0), landing(1), landing(2), landing(3),
+            landing(lay.Z - 1, hb),
+            landing(lay.Z, max(wide - 1, 1), hb),
+            landing(lay.Z, wide, max(wide - 1, 1), hb),
+            landing(lay.Z, runs),
             pltpu.VMEM((2 * nb + 1, nrhs, width), f32),
             pltpu.VMEM((4, most, nrhs, 128), f32),
             state, state, state, state, state, state, state,
             pltpu.SemaphoreType.DMA((2, nb)),
-            pltpu.SemaphoreType.DMA((3, 4, most)),
-            pltpu.SemaphoreType.DMA((3, 4, most)),
-            pltpu.SemaphoreType.DMA((2, 4, most)),
-            pltpu.SemaphoreType.DMA((2, 4, most)),
+            pltpu.SemaphoreType.DMA((4, most)),
+            pltpu.SemaphoreType.DMA((4, most)),
+            *sems,
         ],
         compiler_params=pltpu.CompilerParams(
             collective_id=0, has_side_effects=True, vmem_limit_bytes=60 * 1024 * 1024

time: 171 us -> 145 us (0.85)
  Pallas kernels: 151 us -> 124 us
    pallas_call x1, Pallas kernels: 151 us -> 124 us  [body(): pl.pallas_call(functools.partial(kernel, lay, nb, width, nrhs, blk), out_...]
where the time goes in v3:
time: 145 us
  Pallas kernels  124 us (86%)
  blocking collectives  13.1 us (9%)
  local copies, waits for them, and re-layouts  3.71 us (3%)
  other arithmetic  2.96 us (2%)
    pallas_call x1, Pallas kernels, body(): pl.pallas_call(functools.partial(kernel, lay, nb, width, nrhs, blk), out_...  124 us
    unnamed x1, blocking collectives  13.1 us
    unnamed x6, local copies, waits for them, and re-layouts  3.55 us

profile of v3, /device:TPU:0, one launch (start us, length us, event | category | flops | bytes accessed | tf_op | source)
XLA Modules:
  0.0 144.8 jit_solution(1831783939296235189)
XLA Ops:
  0.0 1.2 dynamic-slice
  1.9 0.7 and_select_fusion.18
  2.6 0.7 bitcast_dynamic-update-slice_fusion
  3.3 13.1 %all-reduce = s32[128]{0:T(128)S(1)} all-reduce(s32[128]{0:T(128)S(1)} %bitcast_dynamic-update-slice_fusion), channel_id=2, replica_groups=mesh['row'=4,'col'=8] {'col'}, use_global_device_ids=true, to_apply=%add | all-reduce | flops 128 | bytes 1024
  16.4 0.2 select_reduce_fusion.2
  16.6 0.7 fusion.9
  17.3 0.1 copy.9
  17.4 0.1 reshape.297.pick_ref
  17.5 0.0 copy-start
  17.5 0.1 select_reduce_fusion
  17.6 0.6 compare_select_fusion.last_ref
  18.2 0.2 select_reduce_fusion.1
  18.3 0.5 compare_select_fusion.1.prev_ref
  18.8 0.0 copy-done
  18.9 124.4 %shard_map.64 = f32[16,2048]{1,0:T(8,128)} custom-call(s32[16]{0:T(128)} %copy-done, s32[16]{0:T(128)} %compare_select_fusion.1.prev_ref, s32[128]{0:T(128)} %compare_select_fusion.last_ref, bf16[8,512,512]{2,1,0:T(8,128)(2,1)} %left_hbm.1, bf16[8,512,512]{2,1,0:T(8,128)(2,1)} %right_hbm.1, f32[16,2048]{1,0:T(8,128)} %b_ref.1, f32[1,2048]{1,0:T(1,128)} %bitcast.16), custom_call_target="tpu_custom_call" | custom-call | tf_op jit(solution)/shard_map/pallas_call | solution.py:429
  143.3 1.6 %copy.12 = f32[16,2048]{1,0:T(8,128)} copy(f32[16,2048]{1,0:T(8,128)} %shard_map.64) | data formatting | bytes 262144
  (3 shorter events, 0.1 us)
Async XLA Ops:
  17.5 1.4 copy-start

commit v4 on v3

--- a/solution.py
+++ b/solution.py
@@ -43,11 +43,12 @@
 
 
 def kernel(
-    lay, nb, width, nrhs, blk,
-    pick_ref, prev_ref, last_ref, left_hbm, right_hbm, b_ref, d_ref, out_ref,
+    lay, nb, width, nrhs, blk, cap,
+    slot_ref, tile_ref, left_hbm, right_hbm, b_ref, d_ref, out_ref,
     lbuf, rbuf, gram, xall, part, r_z, r_near, r_far, r_core, acc, dots,
     v, v_old, sv, y, w, w_old, z,
-    in_sem, dot_send, dot_recv, *sems,
+    tiles, tiles_s, last_v, last_ref, pick_ref, prev_ref,
+    in_sem, dot_send, dot_recv, tile_send, tile_recv, local_sem, *sems,
 ):
     row, col = lax.axis_index("row"), lax.axis_index("col")
     me = lay.coords(row, col)
@@ -190,7 +191,7 @@
                         for o2 in range(1, spans[h][1]):
                             by_far[h, oz, o1, o2].wait_recv()
                     by_core.append(push(group(h, oz), run, ag_core, (h, oz), peer("core", 1)))
-            if hook is not None and t < 4:
+            if hook is not None:
                 hook(t)
             level = {slots - 1: 0, slots: 1, slots + 1: 2}.get(t)
             if level is not None:
@@ -242,7 +243,7 @@
                 def spread(i, carry):
                     for u in range(2):
                         k = at + 2 * i + u
-                        part[k] = acc[last_ref[k]].astype(jnp.bfloat16)
+                        part[k] = acc[last_ref[0, k]].astype(jnp.bfloat16)
                     return carry
 
                 lax.fori_loop(0, run // 2, spread, 0)
@@ -253,7 +254,7 @@
 
         def total(h, oz, o1, o2, i):
             at = place(h, oz, o1, o2) + i
-            value = acc[last_ref[at]] + r_core[h, oz, at - group(h, oz)].astype(jnp.float32)
+            value = acc[last_ref[0, at]] + r_core[h, oz, at - group(h, oz)].astype(jnp.float32)
             if o2 == 0:
                 for o in range(1, spans[h][1]):
                     value = value + r_far[h, oz, o1, o - 1, i].astype(jnp.float32)
@@ -328,9 +329,60 @@
 
         lax.fori_loop(level * nb // 4, (level + 1) * nb // 4, one, 0)
 
+    def send_tiles(axis, ref):
+        copies = []
+        for o in range(1, lay.size[axis]):
+            copies.append(
+                send(ref, ref, (tile_send, tile_recv), (int(axis == "x"), o), peer(axis, o))
+            )
+        return copies
+
+    def place_blocks():
+        load = pltpu.make_async_copy(tiles, tiles_s, local_sem.at[0])
+        load.start()
+        load.wait()
+        rows, cols = lay.Y * CORES, lay.X * lay.Z
+        span = rows * blk
+        target = []
+        for i in range(nb):
+            slot = slot_ref[i]
+            owner = slot // cap % cols
+            position = tiles_s[owner % lay.X, owner // lay.X, 0, slot % cap]
+            row_block, local = position // span, position % span
+            target.append(lay.block(row, row_block // blk, row_block % blk))
+            target.append(lay.block(local // blk, owner, local % blk))
+        number = lax.broadcasted_iota(jnp.int32, last_v.shape, 1)
+        last = jnp.full(last_v.shape, 2 * nb, jnp.int32)
+        for j, at in enumerate(target):
+            pick_ref[j] = at
+            before = jnp.int32(2 * nb)
+            for i in range(j):
+                before = jnp.where(target[i] == at, i, before)
+            prev_ref[j] = before
+            last = jnp.where(number == at, j, last)
+        last_v[...] = last
+        store = pltpu.make_async_copy(last_v, last_ref, local_sem.at[1])
+        store.start()
+        store.wait()
+
+    tiles[me["x"], me["z"]] = tile_ref[...]
+    pending = [send_tiles("z", tiles.at[me["x"], me["z"]])]
+
+    def prepare(t):
+        if t < 4:
+            make_grams(t)
+        if t == 1:
+            for copy in pending.pop():
+                copy.wait()
+            pending.append(send_tiles("x", tiles.at[me["x"]]))
+        if t == 3:
+            for copy in pending.pop():
+                copy.wait()
+            place_blocks()
+
     b = b_ref[...]
     put_dots(b * b, d_ref[...] * b * b)
-    total = gather(b_ref, make_grams)
+    total = gather(b_ref, prepare)
     first = pick_dot(total, 0)
     beta = jnp.sqrt(first)
     sigma = pick_dot(total, 1) / first
@@ -391,25 +443,7 @@
     blk = own // width
     lay = Layout(rows, cols, blk)
     cap = tile_pos.shape[-1]
-    band_pos = lax.all_gather(tile_pos.reshape(-1), "col", axis=0, tiled=True)
-    owner = bundle_tile_slot // cap % cols
-    wanted = bundle_tile_slot % (cap * cols)
-    hit = wanted[:, None] == jnp.arange(cap * cols, dtype=jnp.int32)[None, :]
-    position = jnp.sum(jnp.where(hit, band_pos[None, :], 0), axis=1)
-    span = rows * blk
-    row_block, local = position // span, position % span
-    at_row = lay.block(lax.axis_index("row"), row_block // blk, row_block % blk)
-    at_col = lay.block(local // blk, owner, local % blk)
-    target = jnp.stack([at_row, at_col], axis=1).reshape(-1)
-    number = jnp.arange(2 * nb, dtype=jnp.int32)
-    same = (target[:, None] == target[None, :]) & (number[None, :] < number[:, None])
-    prev = jnp.max(jnp.where(same, number[None, :], -1), axis=1)
-    prev = jnp.where(prev < 0, 2 * nb, prev)
     blocks = blk * rows * cols
-    found = target[None, :] == jnp.arange(blocks, dtype=jnp.int32)[:, None]
-    last = jnp.max(jnp.where(found, number[None, :], -1), axis=1)
-    last = jnp.where(last < 0, 2 * nb, last)
-
     hb = lay.hb
     bf16, f32 = jnp.bfloat16, jnp.float32
     most = max(lay.size.values())
@@ -427,9 +461,9 @@
     hbm = pl.BlockSpec(memory_space=pl.ANY)
     state = pltpu.VMEM((nrhs, own), f32)
     return pl.pallas_call(
-        functools.partial(kernel, lay, nb, width, nrhs, blk),
+        functools.partial(kernel, lay, nb, width, nrhs, blk, cap),
         out_shape=jax.ShapeDtypeStruct((nrhs, own), f32),
-        in_specs=[smem, smem, smem, hbm, hbm, vmem, vmem],
+        in_specs=[smem, vmem, hbm, hbm, vmem, vmem],
         out_specs=vmem,
         scratch_shapes=[
             pltpu.VMEM((nb, measures, width), bf16),
@@ -444,15 +478,27 @@
             pltpu.VMEM((2 * nb + 1, nrhs, width), f32),
             pltpu.VMEM((4, most, nrhs, 128), f32),
             state, state, state, state, state, state, state,
+            pltpu.VMEM((lay.X, lay.Z, 1, cap), jnp.int32),
+            pltpu.SMEM((lay.X, lay.Z, 1, cap), jnp.int32),
+            pltpu.VMEM((1, blocks), jnp.int32),
+            pltpu.SMEM((1, blocks), jnp.int32),
+            pltpu.SMEM((2 * nb,), jnp.int32),
+            pltpu.SMEM((2 * nb,), jnp.int32),
             pltpu.SemaphoreType.DMA((2, nb)),
             pltpu.SemaphoreType.DMA((4, most)),
             pltpu.SemaphoreType.DMA((4, most)),
+            pltpu.SemaphoreType.DMA((2, most)),
+            pltpu.SemaphoreType.DMA((2, most)),
+            pltpu.SemaphoreType.DMA((2,)),
             *sems,
         ],
         compiler_params=pltpu.CompilerParams(
             collective_id=0, has_side_effects=True, vmem_limit_bytes=60 * 1024 * 1024
         ),
-    )(target, prev, last, left, right, right_sides, diagonal.reshape(1, own))
+    )(
+        bundle_tile_slot, tile_pos.reshape(1, cap), left, right, right_sides,
+        diagonal.reshape(1, own),
+    )
 
 
 def solution(mesh):

time: 145 us -> 133 us (0.917)
  blocking collectives: 13.1 us -> 0 us
  Pallas kernels: 124 us -> 131 us
  other arithmetic: 2.96 us -> 0 us
  local copies, waits for them, and re-layouts: 3.71 us -> 1.57 us
    unnamed x1 -> x0, blocking collectives: 13.1 us -> none
    pallas_call x1, Pallas kernels: 124 us -> 131 us  [body(): pl.pallas_call(functools.partial(kernel, lay, nb, width, nrhs, blk, cap),...]
    unnamed x6 -> x1, local copies, waits for them, and re-layouts: 3.55 us -> 1.57 us
    select_n x3 -> x0, other arithmetic: 1.76 us -> none  [the longest x1 0.67 us: body(): wanted = bundle_tile_slot % (cap * cols)]
where the time goes in v4:
time: 133 us
  Pallas kernels  131 us (98%)
  local copies, waits for them, and re-layouts  1.57 us (1%)
    pallas_call x1, Pallas kernels, body(): pl.pallas_call(functools.partial(kernel, lay, nb, width, nrhs, blk, cap),...  131 us

profile of v4, /device:TPU:0, one launch (start us, length us, event | category | flops | bytes accessed | tf_op | source)
XLA Modules:
  0.0 132.8 jit_solution(9886258829535319282)
XLA Ops:
  0.0 131.2 %shard_map.64 = f32[16,2048]{1,0:T(8,128)} custom-call(s32[8]{0:T(128)} %slot_ref.1, s32[1,16]{1,0:T(1,128)} %bitcast.3, bf16[8,512,512]{2,1,0:T(8,128)(2,1)} %left_hbm.1, bf16[8,512,512]{2,1,0:T(8,128)(2,1)} %right_hbm.1, f32[16,2048]{1,0:T(8,128)} %b_ref.1, f32[1,2048]{1,0:T(1,128)} %bitcast.2), custom_call_target="tpu_custom_call" | custom-call | tf_op jit(solution)/shard_map/pallas_call | solution.py:463
  131.2 1.6 %copy.8 = f32[16,2048]{1,0:T(8,128)} copy(f32[16,2048]{1,0:T(8,128)} %shard_map.64) | data formatting | bytes 262144

commit v5 on v4

--- a/solution.py
+++ b/solution.py
@@ -218,19 +218,16 @@
     def products():
         acc[2 * nb] = jnp.zeros((nrhs, width), jnp.float32)
 
-        def one(i, carry):
+        for i in range(nb):
             g = gram[i]
             x_row = xall[pick_ref[2 * i]]
             x_col = xall[pick_ref[2 * i + 1]]
-            row_term = lax.dot_general(
+            acc[2 * i] = lax.dot_general(
                 x_col, g, (((1,), (1,)), ((), ())), preferred_element_type=jnp.float32
             )
-            col_term = jnp.dot(x_row, g, preferred_element_type=jnp.float32)
-            acc[2 * i] = row_term + acc[prev_ref[2 * i]]
-            acc[2 * i + 1] = col_term + acc[prev_ref[2 * i + 1]]
-            return carry
-
-        lax.fori_loop(0, nb, one, 0)
+            acc[2 * i + 1] = jnp.dot(x_row, g, preferred_element_type=jnp.float32)
+        for j in range(1, 2 * nb):
+            acc[j] = acc[j] + acc[prev_ref[j]]
 
     def scatter_sum():
         sent = []
@@ -375,7 +372,7 @@
             for copy in pending.pop():
                 copy.wait()
             pending.append(send_tiles("x", tiles.at[me["x"]]))
-        if t == 3:
+        if t == lay.Z + 1:
             for copy in pending.pop():
                 copy.wait()
             place_blocks()

time: 133 us -> 129 us (0.970)
  Pallas kernels: 131 us -> 127 us
    pallas_call x1, Pallas kernels: 131 us -> 127 us  [body(): pl.pallas_call(functools.partial(kernel, lay, nb, width, nrhs, blk, cap),...]
where the time goes in v5:
time: 129 us
  Pallas kernels  127 us (98%)
  local copies, waits for them, and re-layouts  1.57 us (1%)
    pallas_call x1, Pallas kernels, body(): pl.pallas_call(functools.partial(kernel, lay, nb, width, nrhs, blk, cap),...  127 us

profile of v5, /device:TPU:0, one launch (start us, length us, event | category | flops | bytes accessed | tf_op | source)
XLA Modules:
  0.0 129.0 jit_solution(15204774297355031850)
XLA Ops:
  0.0 127.4 %shard_map.64 = f32[16,2048]{1,0:T(8,128)} custom-call(s32[8]{0:T(128)} %slot_ref.1, s32[1,16]{1,0:T(1,128)} %bitcast.3, bf16[8,512,512]{2,1,0:T(8,128)(2,1)} %left_hbm.1, bf16[8,512,512]{2,1,0:T(8,128)(2,1)} %right_hbm.1, f32[16,2048]{1,0:T(8,128)} %b_ref.1, f32[1,2048]{1,0:T(1,128)} %bitcast.2), custom_call_target="tpu_custom_call" | custom-call | tf_op jit(solution)/shard_map/pallas_call | solution.py:460
  127.4 1.6 %copy.8 = f32[16,2048]{1,0:T(8,128)} copy(f32[16,2048]{1,0:T(8,128)} %shard_map.64) | data formatting | bytes 262144
